TPU v7x, 32 devices: a whole 2x2x4 slice. The times are simulated.
32 devices in a mesh: rep: 8 (over z, core), shard: 4 (over y, x).
Axes of the slice: x: 2, y: 2, z: 4, core: 2. Of those that a mesh axis runs over, the one named last changes fastest.
Arguments:
- tokens: bfloat16 [32, 1024, 1024], P(('rep', 'shard')), may hold values from -6 to 6
- segments: int32 [32, 1024], P(('rep', 'shard')), may hold values from 0 to 7, never falling along the last dimension, each value on 1 to 512 neighbouring positions
- cotangent: bfloat16 [32, 1024, 1024], P(('rep', 'shard')), may hold values from -6 to 6
- norm_mix: bfloat16 [1024], P('shard'), may hold values from 0.5 to 1.5
- w_query: bfloat16 [1024, 512], P('shard'), may hold values from -0.1875 to 0.1875
- w_key: bfloat16 [1024, 512], P('shard'), may hold values from -0.1875 to 0.1875
- w_value: bfloat16 [1024, 1024], P('shard'), may hold values from -0.1875 to 0.1875
- w_outgate: bfloat16 [1024, 1024], P('shard'), may hold values from -0.1875 to 0.1875
- w_low: bfloat16 [1024, 16], P('shard'), may hold values from -0.1875 to 0.1875
- w_high: bfloat16 [16, 512], P(None, 'shard'), may hold values from -1.5 to 1.5
- decay_bias: bfloat16 [512], P('shard'), may hold values from 0.5 to 4.5
- head_gain: bfloat16 [256], P('shard'), may hold values from 0.5 to 1.5
- w_out: bfloat16 [1024, 1024], P('shard'), may hold values from -0.1875 to 0.1875
- norm_mlp: bfloat16 [1024], P('shard'), may hold values from 0.5 to 1.5
- w_gate: bfloat16 [1024, 2816], P('shard'), may hold values from -0.1875 to 0.1875
- w_up: bfloat16 [1024, 2816], P('shard'), may hold values from -0.1875 to 0.1875
- w_down: bfloat16 [2816, 1024], P('shard'), may hold values from -0.109375 to 0.109375
Outputs:
- block_out: bfloat16 [32, 1024, 1024], P(('rep', 'shard'))
- grad_tokens: float32 [32, 1024, 1024], P(('rep', 'shard'))
- grad_norm_mix: float32 [1024], P('shard')
- grad_w_query: float32 [1024, 512], P('shard')
- grad_w_key: float32 [1024, 512], P('shard')
- grad_w_value: float32 [1024, 1024], P('shard')
- grad_w_outgate: float32 [1024, 1024], P('shard')
- grad_w_low: float32 [1024, 16], P('shard')
- grad_w_high: float32 [16, 512], P(None, 'shard')
- grad_decay_bias: float32 [512], P('shard')
- grad_head_gain: float32 [256], P('shard')
- grad_w_out: float32 [1024, 1024], P('shard')
- grad_norm_mlp: float32 [1024], P('shard')
- grad_w_gate: float32 [1024, 2816], P('shard')
- grad_w_up: float32 [1024, 2816], P('shard')
- grad_w_down: float32 [2816, 1024], P('shard')
Inputs may be any that keep to these rules, and one draw needn't show every extreme that they name: `segments`: segment numbers never fall along a sequence; a document has 1 to 512 tokens and some document has exactly 512.
All inputs are finite; a program needn't handle non-finite values.
Results may differ from a plain program's by a relative error of at most 0.018.
Values may be sent and summed in bfloat16 or wider, within the bound.
A program may use at most 256 MiB of HBM per device.

v0:
```python
from functools import partial
import jax
import jax.numpy as jnp
from jax import lax
from jax.sharding import PartitionSpec as P

HEADS = 4
KH = 128
VH = 256
BLOCK = 64
VD = 1024
HEAD_EPS = 1.0


def matmul(left, right):
    return jnp.dot(left, right, preferred_element_type=jnp.float32)


def left_trans(left, right):
    return lax.dot_general(
        left, right, (((0,), (0,)), ((), ())), preferred_element_type=jnp.float32
    )


def right_trans(left, right):
    return lax.dot_general(
        left, right, (((1,), (1,)), ((), ())), preferred_element_type=jnp.float32
    )


def rms_scale(values, gain, epsilon=1e-05):
    inverse = lax.rsqrt(jnp.mean(values * values, axis=-1, keepdims=True) + epsilon)
    return values * inverse * gain


def block_pass(query, keys, values, decay, segment):
    length, heads, key_size = query.shape
    value_size = values.shape[-1]
    blocks = length // BLOCK
    query = query * key_size ** (-0.5)
    lower = lax.broadcasted_iota(jnp.int32, (BLOCK, BLOCK), 0) >= lax.broadcasted_iota(
        jnp.int32, (BLOCK, BLOCK), 1
    )

    def advance(carry, item):
        state, last_seg = carry
        qblk, kblk, vblk, dblk, sblk = item
        cumul = jnp.cumsum(dblk, axis=0)
        q_scaled = qblk * jnp.exp(cumul)
        k_scaled = kblk * jnp.exp(-cumul)
        same = ((sblk[:, None] == sblk[None, :]) & lower).astype(jnp.float32)
        scores = (
            jnp.einsum("thd,shd->hts", q_scaled, k_scaled, precision=lax.Precision.HIGHEST)
            * same[None]
        )
        inner = jnp.einsum("hts,she->the", scores, vblk, precision=lax.Precision.HIGHEST)
        keep = (sblk == last_seg).astype(jnp.float32)
        carried = (
            jnp.einsum("thd,hde->the", q_scaled, state, precision=lax.Precision.HIGHEST)
            * keep[:, None, None]
        )
        final = cumul[-1]
        tail = (sblk == sblk[-1]).astype(jnp.float32)
        scaled = k_scaled * jnp.exp(final)[None] * tail[:, None, None]
        fresh = jnp.einsum("shd,she->hde", scaled, vblk, precision=lax.Precision.HIGHEST)
        stay = (sblk[-1] == last_seg).astype(jnp.float32)
        state = jnp.exp(final)[:, :, None] * state * stay + fresh
        return ((state, sblk[-1]), inner + carried)

    def shaped(array):
        return array.reshape((blocks, BLOCK) + array.shape[1:])

    start = (jnp.zeros((heads, key_size, value_size), jnp.float32), jnp.int32(-1))
    _, outputs = lax.scan(
        jax.checkpoint(advance),
        start,
        (shaped(query), shaped(keys), shaped(values), shaped(decay), shaped(segment)),
    )
    return outputs.reshape(length, heads, value_size)


def mixer_core(query, keys, values, outgate, lowpre, decay_bias, head_gain, segment):
    total = query.shape[0]
    seqs = segment.shape[0]
    length = segment.shape[1]
    decay = jax.nn.log_sigmoid(lowpre + decay_bias) / 16.0

    def split(array, width):
        return array.reshape(seqs, length, HEADS, width)

    mixed = jax.vmap(block_pass)(
        split(query, KH), split(keys, KH), split(values, VH), split(decay, KH), segment
    )
    normed = rms_scale(mixed, head_gain, HEAD_EPS)
    return normed.reshape(total, VD) * jax.nn.silu(outgate)


def local(
    tokens,
    segments,
    cotangent,
    norm_mix,
    w_query,
    w_key,
    w_value,
    w_outgate,
    w_low,
    w_high,
    decay_bias,
    head_gain,
    w_out,
    norm_mlp,
    w_gate,
    w_up,
    w_down,
):
    mixer_full = (
        lax.all_gather(norm_mix, "shard", axis=0, tiled=True),
        lax.all_gather(w_query, "shard", axis=0, tiled=True),
        lax.all_gather(w_key, "shard", axis=0, tiled=True),
        lax.all_gather(w_value, "shard", axis=0, tiled=True),
        lax.all_gather(w_outgate, "shard", axis=0, tiled=True),
        lax.all_gather(w_low, "shard", axis=0, tiled=True),
        lax.all_gather(w_high, "shard", axis=1, tiled=True),
        lax.all_gather(decay_bias, "shard", axis=0, tiled=True),
        lax.all_gather(head_gain, "shard", axis=0, tiled=True),
        lax.all_gather(w_out, "shard", axis=0, tiled=True),
    )
    feed_full = (
        lax.all_gather(norm_mlp, "shard", axis=0, tiled=True),
        lax.all_gather(w_gate, "shard", axis=0, tiled=True),
        lax.all_gather(w_up, "shard", axis=0, tiled=True),
        lax.all_gather(w_down, "shard", axis=0, tiled=True),
    )
    gain_mix, query_w, key_w, value_w, outgate_w, low_w, high_w, bias_w, headgain_w, out_w = (
        mixer_full
    )
    gain_feed, gate_w, up_w, down_w = feed_full
    total = tokens.shape[0] * tokens.shape[1]
    width = tokens.shape[2]
    inputs = tokens.reshape(total, width).astype(jnp.float32)
    normed_mix, mix_pull = jax.vjp(rms_scale, inputs, gain_mix.astype(jnp.float32))
    first = normed_mix.astype(jnp.bfloat16)
    query = matmul(first, query_w)
    keys = matmul(first, key_w)
    values = matmul(first, value_w)
    outgate = matmul(first, outgate_w)
    lowrank = matmul(first, low_w).astype(jnp.bfloat16)
    lowpre = matmul(lowrank, high_w)
    core_local = partial(mixer_core, segment=segments)
    mixed, core_pull = jax.vjp(
        core_local,
        query,
        keys,
        values,
        outgate,
        lowpre,
        bias_w.astype(jnp.float32),
        headgain_w.astype(jnp.float32),
    )
    mixed_low = mixed.astype(jnp.bfloat16)
    resid = inputs + matmul(mixed_low, out_w)
    normed_feed, feed_pull = jax.vjp(rms_scale, resid, gain_feed.astype(jnp.float32))
    second = normed_feed.astype(jnp.bfloat16)
    gate = matmul(second, gate_w)
    upward = matmul(second, up_w)
    sigma = jax.nn.sigmoid(gate)
    swish = gate * sigma
    hidden = (swish * upward).astype(jnp.bfloat16)
    result = (resid + matmul(hidden, down_w)).astype(jnp.bfloat16)
    feed_back = (
        lax.all_gather(norm_mlp, "shard", axis=0, tiled=True),
        lax.all_gather(w_gate, "shard", axis=0, tiled=True),
        lax.all_gather(w_up, "shard", axis=0, tiled=True),
        lax.all_gather(w_down, "shard", axis=0, tiled=True),
    )
    unused_gain, back_gate, back_up, back_down = feed_back
    grad_out = cotangent.reshape(total, width)
    part_down = left_trans(hidden, grad_out)
    grad_hidden = right_trans(grad_out, back_down)
    slope = sigma * (1.0 + gate * (1.0 - sigma))
    grad_gate = (grad_hidden * upward * slope).astype(jnp.bfloat16)
    grad_up = (grad_hidden * swish).astype(jnp.bfloat16)
    part_gate = left_trans(second, grad_gate)
    part_up = left_trans(second, grad_up)
    grad_second = right_trans(grad_gate, back_gate) + right_trans(grad_up, back_up)
    grad_resid_norm, part_norm_mlp = feed_pull(grad_second)
    grad_resid = grad_out.astype(jnp.float32) + grad_resid_norm
    grad_branch = grad_resid.astype(jnp.bfloat16)
    mixer_back = (
        lax.all_gather(norm_mix, "shard", axis=0, tiled=True),
        lax.all_gather(w_query, "shard", axis=0, tiled=True),
        lax.all_gather(w_key, "shard", axis=0, tiled=True),
        lax.all_gather(w_value, "shard", axis=0, tiled=True),
        lax.all_gather(w_outgate, "shard", axis=0, tiled=True),
        lax.all_gather(w_low, "shard", axis=0, tiled=True),
        lax.all_gather(w_high, "shard", axis=1, tiled=True),
        lax.all_gather(decay_bias, "shard", axis=0, tiled=True),
        lax.all_gather(head_gain, "shard", axis=0, tiled=True),
        lax.all_gather(w_out, "shard", axis=0, tiled=True),
    )
    (
        unused_mix,
        back_query,
        back_key,
        back_value,
        back_outgate,
        back_low,
        back_high,
        unused_bias,
        unused_headgain,
        back_out,
    ) = mixer_back
    part_out = left_trans(mixed_low, grad_branch)
    grad_mixed = right_trans(grad_branch, back_out)
    grad_query, grad_keys, grad_values, grad_outgate, grad_lowpre, part_bias, part_headgain = (
        core_pull(grad_mixed)
    )
    grad_query = grad_query.astype(jnp.bfloat16)
    grad_keys = grad_keys.astype(jnp.bfloat16)
    grad_values = grad_values.astype(jnp.bfloat16)
    grad_outgate = grad_outgate.astype(jnp.bfloat16)
    grad_lowpre = grad_lowpre.astype(jnp.bfloat16)
    part_high = left_trans(lowrank, grad_lowpre)
    grad_lowrank = right_trans(grad_lowpre, back_high).astype(jnp.bfloat16)
    part_low = left_trans(first, grad_lowrank)
    part_query = left_trans(first, grad_query)
    part_key = left_trans(first, grad_keys)
    part_value = left_trans(first, grad_values)
    part_outgate = left_trans(first, grad_outgate)
    grad_first = (
        right_trans(grad_query, back_query)
        + right_trans(grad_keys, back_key)
        + right_trans(grad_values, back_value)
    )
    grad_first = (
        grad_first + right_trans(grad_outgate, back_outgate) + right_trans(grad_lowrank, back_low)
    )
    grad_inputs_norm, part_norm_mix = mix_pull(grad_first)
    grad_inputs = (grad_resid + grad_inputs_norm).reshape(tokens.shape)
    feed_rows = (
        lax.psum_scatter(
            part_norm_mlp.astype(jnp.bfloat16), "shard", scatter_dimension=0, tiled=True
        ).astype(jnp.float32),
        lax.psum_scatter(
            part_gate.astype(jnp.bfloat16), "shard", scatter_dimension=0, tiled=True
        ).astype(jnp.float32),
        lax.psum_scatter(
            part_up.astype(jnp.bfloat16), "shard", scatter_dimension=0, tiled=True
        ).astype(jnp.float32),
        lax.psum_scatter(
            part_down.astype(jnp.bfloat16), "shard", scatter_dimension=0, tiled=True
        ).astype(jnp.float32),
    )
    feed_sums = (
        lax.psum(feed_rows[0].astype(jnp.bfloat16), "rep").astype(jnp.float32),
        lax.psum(feed_rows[1].astype(jnp.bfloat16), "rep").astype(jnp.float32),
        lax.psum(feed_rows[2].astype(jnp.bfloat16), "rep").astype(jnp.float32),
        lax.psum(feed_rows[3].astype(jnp.bfloat16), "rep").astype(jnp.float32),
    )
    mixer_rows = (
        lax.psum_scatter(
            part_norm_mix.astype(jnp.bfloat16), "shard", scatter_dimension=0, tiled=True
        ).astype(jnp.float32),
        lax.psum_scatter(
            part_query.astype(jnp.bfloat16), "shard", scatter_dimension=0, tiled=True
        ).astype(jnp.float32),
        lax.psum_scatter(
            part_key.astype(jnp.bfloat16), "shard", scatter_dimension=0, tiled=True
        ).astype(jnp.float32),
        lax.psum_scatter(
            part_value.astype(jnp.bfloat16), "shard", scatter_dimension=0, tiled=True
        ).astype(jnp.float32),
        lax.psum_scatter(
            part_outgate.astype(jnp.bfloat16), "shard", scatter_dimension=0, tiled=True
        ).astype(jnp.float32),
        lax.psum_scatter(
            part_low.astype(jnp.bfloat16), "shard", scatter_dimension=0, tiled=True
        ).astype(jnp.float32),
        lax.psum_scatter(
            part_high.astype(jnp.bfloat16), "shard", scatter_dimension=1, tiled=True
        ).astype(jnp.float32),
        lax.psum_scatter(
            part_bias.astype(jnp.bfloat16), "shard", scatter_dimension=0, tiled=True
        ).astype(jnp.float32),
        lax.psum_scatter(
            part_headgain.astype(jnp.bfloat16), "shard", scatter_dimension=0, tiled=True
        ).astype(jnp.float32),
        lax.psum_scatter(
            part_out.astype(jnp.bfloat16), "shard", scatter_dimension=0, tiled=True
        ).astype(jnp.float32),
    )
    mixer_sums = (
        lax.psum(mixer_rows[0].astype(jnp.bfloat16), "rep").astype(jnp.float32),
        lax.psum(mixer_rows[1].astype(jnp.bfloat16), "rep").astype(jnp.float32),
        lax.psum(mixer_rows[2].astype(jnp.bfloat16), "rep").astype(jnp.float32),
        lax.psum(mixer_rows[3].astype(jnp.bfloat16), "rep").astype(jnp.float32),
        lax.psum(mixer_rows[4].astype(jnp.bfloat16), "rep").astype(jnp.float32),
        lax.psum(mixer_rows[5].astype(jnp.bfloat16), "rep").astype(jnp.float32),
        lax.psum(mixer_rows[6].astype(jnp.bfloat16), "rep").astype(jnp.float32),
        lax.psum(mixer_rows[7].astype(jnp.bfloat16), "rep").astype(jnp.float32),
        lax.psum(mixer_rows[8].astype(jnp.bfloat16), "rep").astype(jnp.float32),
        lax.psum(mixer_rows[9].astype(jnp.bfloat16), "rep").astype(jnp.float32),
    )
    return (
        result.reshape(tokens.shape),
        grad_inputs,
        mixer_sums[0],
        mixer_sums[1],
        mixer_sums[2],
        mixer_sums[3],
        mixer_sums[4],
        mixer_sums[5],
        mixer_sums[6],
        mixer_sums[7],
        mixer_sums[8],
        mixer_sums[9],
        feed_sums[0],
        feed_sums[1],
        feed_sums[2],
        feed_sums[3],
    )


def solution(mesh):
    in_specs = (
        P(("rep", "shard"), None, None),
        P(("rep", "shard"), None),
        P(("rep", "shard"), None, None),
        P("shard"),
        P("shard", None),
        P("shard", None),
        P("shard", None),
        P("shard", None),
        P("shard", None),
        P(None, "shard"),
        P("shard"),
        P("shard"),
        P("shard", None),
        P("shard"),
        P("shard", None),
        P("shard", None),
        P("shard", None),
    )
    out_specs = (
        P(("rep", "shard"), None, None),
        P(("rep", "shard"), None, None),
        P("shard"),
        P("shard", None),
        P("shard", None),
        P("shard", None),
        P("shard", None),
        P("shard", None),
        P(None, "shard"),
        P("shard"),
        P("shard"),
        P("shard", None),
        P("shard"),
        P("shard", None),
        P("shard", None),
        P("shard", None),
    )
    return jax.shard_map(local, mesh=mesh, in_specs=in_specs, out_specs=out_specs, check_vma=False)
```

profile of v0, /device:TPU:0, one launch (start us, length us, event | category | flops | bytes accessed | tf_op | source)
XLA Modules:
  0.0 1311.7 jit_solution(10404058792352158195)
XLA Ops:
  19.0 9.5 all-gather
  67.3 8.9 all-reduce.1
  115.7 177.9 %while.44 = (s32[]{:T(128)}, f32[1,4,128,256]{3,2,1,0:T(8,128)S(1)}, s32[1]{0:T(128)}, f32[16,1,64,4,256]{4,2,3,1,0:T(8,128)}, f32[16,1,4,128,256]{4,3,2,1,0:T(8...) while((s32[]{:T(128)}, ...), condition=%wide.region_3.4_spmd.clone.clone, body=%wide.region_1.3_spmd.clone.sunk.clone | while | flops 280002816 | bytes 6207163 | solution.py:74
  309.2 8.6 multiply_convert_fusion.4
  326.5 11.6 fusion.159
  338.1 12.9 fusion.160
  351.0 31.2 %all-gather.26.cloned.1.call-done = bf16[2816,1024]{1,0:T(8,128)(2,1)} async-done(((bf16[704,1024]{1,0:T(8,128)(2,1)}), bf16[2816,1024]{1,0:T(8,128)(2,1)}) %all-gather.26.cloned.1.call-update) | async-done | bytes 5767184 | tf_op jit(solution)/shard_map/all_gather | solution.py:133
  382.2 21.6 %multiply_convert_fusion = (bf16[1024,2816]{1,0:T(8,128)(2,1)}, bf16[1024,2816]{1,0:T(8,128)(2,1)}, bf16[1024,2816]{1,0:T(8,128)(2,1)}) fusion(f32[1024,2816]{1,0:T(8,128)} %fusion.159, f32[1024,2816]{1,0:T(8,128)} %fusion.160, bf16[2816,1024]{1,0:T(8,128)(2,1)} %all-gather.26.cloned.1.call-done, bf16[1,1024,1024]{2,1,0:T(8,128)(2,1)S(1)} %copy-done.19), kind=kOutput, calls=%fused_computation.120 | convolution fusion | flops 5948833792 | bytes 48234496 | tf_op jit(solution)/shard_map/dot_general | solution.py:26
  403.8 10.2 fusion.161
  449.8 259.2 %while.45 = (s32[]{:T(128)}, f32[1,4,128,256]{2,3,1,0:T(8,128)S(1)}, f32[16,1,64,4,128]{4,2,3,1,0:T(8,128)}, bf16[16,1,64,4,128]{4,2,3,1,0:T(8,128)(2,1)}, bf16[...) while((s32[]{:T(128)}, ...), condition=%wide.region_13.14_spmd.clone.clone, body=%wide.region_8.13_spmd.clone.sunk.clone | while | flops 585089280 | bytes 16077553 | solution.py:74
  739.9 10.9 convolution_convert_fusion.2
  750.9 11.1 convolution_convert_fusion.1
  762.3 11.1 convolution_convert_fusion
  811.7 38.9 %reduce-scatter.17.cloned.1.call-done = bf16[256,1024]{1,0:T(8,128)(2,1)} async-done(((bf16[1024,1024]{1,0:T(8,128)(2,1)}), bf16[256,1024]{1,0:T(8,128)(2,1)}) %reduce-scatter.17.cloned.1.call-update) | async-done | bytes 524304 | tf_op jit(solution)/shard_map/reduce_scatter | solution.py:271
  850.6 38.2 %reduce-scatter.19.cloned.1.call-done = bf16[256,1024]{1,0:T(8,128)(2,1)} async-done(((bf16[1024,1024]{1,0:T(8,128)(2,1)}), bf16[256,1024]{1,0:T(8,128)(2,1)}) %reduce-scatter.19.cloned.1.call-update) | async-done | bytes 524304 | tf_op jit(solution)/shard_map/reduce_scatter | solution.py:274
  888.8 69.0 %reduce-scatter.25.cloned.1.call-done = bf16[256,2816]{1,0:T(8,128)(2,1)} async-done(((bf16[1024,2816]{1,0:T(8,128)(2,1)}), bf16[256,2816]{1,0:T(8,128)(2,1)}) %reduce-scatter.25.cloned.1.call-update) | async-done | bytes 1441808 | tf_op jit(solution)/shard_map/reduce_scatter | solution.py:245
  957.8 68.9 %reduce-scatter.27.cloned.1.call-done = bf16[256,2816]{1,0:T(8,128)(2,1)} async-done(((bf16[1024,2816]{1,0:T(8,128)(2,1)}), bf16[256,2816]{1,0:T(8,128)(2,1)}) %reduce-scatter.27.cloned.1.call-update) | async-done | bytes 1441808 | tf_op jit(solution)/shard_map/reduce_scatter | solution.py:248
  1026.7 68.9 %reduce-scatter.29.cloned.1.call-done = bf16[704,1024]{1,0:T(8,128)(2,1)} async-done(((bf16[2816,1024]{1,0:T(8,128)(2,1)}), bf16[704,1024]{1,0:T(8,128)(2,1)}) %reduce-scatter.29.cloned.1.call-update) | async-done | bytes 1441808 | tf_op jit(solution)/shard_map/reduce_scatter | solution.py:251
  1095.7 8.9 fusion.90
  1104.6 9.4 all-reduce.8
  1126.0 10.6 fusion.102
  1140.1 8.4 reduce-scatter.21.cloned.1.call-done
  1148.5 29.1 %all-reduce.6 = (bf16[256]{0:T(256)(128)(2,1)S(1)}, bf16[256,16]{0,1:T(8,128)(2,1)S(1)}, bf16[16,128]{1,0:T(8,128)(2,1)S(1)}, bf16[128]{0:T(256)(128)(2,1)S(1)},...) all-reduce(bf16[256]{0:T(256)(128)(2,1)S(1)} %dynamic-slice.2, ...), channel_id=1, replica_groups=mesh['rep'=8,'shard'=4] {'rep'}, use_global_device_ids=true, to_apply=%region_17.18 | all-reduce | flops 6848 | bytes 27392 | tf_op jit(solution)/shard_map/psum | solution.py:294
  1181.0 112.0 %all-reduce.11.cloned.1.call-done = (bf16[256,512]{1,0:T(8,128)(2,1)}, bf16[256,512]{1,0:T(8,128)(2,1)}, bf16[256,1024]{1,0:T(8,128)(2,1)}, bf16[256,1024]{1,0:T...) async-done(((bf16[256,512]{1,0:T(8,128)(2,1)}, bf16[256,512]{1,0:T(8,128)(2,1)}, ...) | async-done | bytes 6422544 | tf_op jit(solution)/shard_map/psum | solution.py:295
  (1001 shorter events, 640.1 us)
Async XLA Ops:
  7.2 81.0 %all-gather.12.cloned.1.call-start = ((), (), s32[]{:S(2)}) async-start(), calls=%async_computation.10 | async-start | bytes 1310720 | tf_op jit(solution)/shard_map/all_gather | solution.py:120
  7.9 82.5 %all-gather.16.cloned.1.call-start = ((), (), s32[]{:S(2)}) async-start(), calls=%async_computation.12 | async-start | bytes 1310720 | tf_op jit(solution)/shard_map/all_gather | solution.py:119
  8.7 96.6 %all-gather.14.cloned.1.call-start = ((), (), s32[]{:S(2)}) async-start(), calls=%async_computation.11 | async-start | bytes 2621440 | tf_op jit(solution)/shard_map/all_gather | solution.py:121
  9.4 299.8 %all-gather.18.cloned.1.call-start = ((), (), s32[]{:S(2)}) async-start(), calls=%async_computation.13 | async-start | bytes 2621440 | tf_op jit(solution)/shard_map/all_gather | solution.py:122
  10.0 307.8 %all-gather.20.cloned.1.call-start = ((), (), s32[]{:S(2)}) async-start(), calls=%async_computation.14 | async-start | bytes 2621440 | tf_op jit(solution)/shard_map/all_gather | solution.py:127
  10.6 314.6 %all-gather.22.cloned.1.call-start = ((), (), s32[]{:S(2)}) async-start(), calls=%async_computation.15 | async-start | bytes 7208960 | tf_op jit(solution)/shard_map/all_gather | solution.py:131
  11.1 327.0 %all-gather.24.cloned.1.call-start = ((), (), s32[]{:S(2)}) async-start(), calls=%async_computation.16 | async-start | bytes 7208960 | tf_op jit(solution)/shard_map/all_gather | solution.py:132
  11.9 370.3 %all-gather.26.cloned.1.call-start = ((), (), s32[]{:S(2)}) async-start(), calls=%async_computation.17 | async-start | bytes 7208960 | tf_op jit(solution)/shard_map/all_gather | solution.py:133
  12.6 791.0 %reduce-scatter.13.cloned.1.call-start = ((), (), s32[]{:S(2)}) async-start(), calls=%async_computation.18 | async-start | bytes 1310720 | tf_op jit(solution)/shard_map/reduce_scatter | solution.py:265
  18.4 299.3 %copy-start.2 = (bf16[1,1024,1024]{1,2,0:T(8,128)(2,1)}, bf16[1,1024,1024]{1,2,0:T(8,128)(2,1)S(1)}, u32[]{:S(2)}) copy-start(bf16[1,1024,1024]{1,2,0:T(8,128)(2,1)S(1)} %copy.180) | copy-start | bytes 6291460
  19.0 290.2 %copy-start.36 = (f32[1024]{0:T(1024)}, f32[1024]{0:T(1024)S(1)}, u32[]{:S(2)}) copy-start(f32[1024]{0:T(1024)S(1)} %fusion.144) | copy-start | bytes 12292
  28.5 280.7 %copy-start.38 = (f32[4,1,256]{2,1,0:T(1,128)}, f32[4,1,256]{2,1,0:T(1,128)S(1)}, u32[]{:S(2)}) copy-start(f32[4,1,256]{2,1,0:T(1,128)S(1)} %convert_element_type.341) | copy-start | bytes 12292
  43.2 54.1 %copy-start.42 = (bf16[1024,16]{0,1:T(8,128)(2,1)}, bf16[1024,16]{0,1:T(8,128)(2,1)S(1)}, u32[]{:S(2)}) copy-start(bf16[1024,16]{0,1:T(8,128)(2,1)S(1)} %convolution_convert_fusion.5) | copy-start | bytes 98308
  714.3 89.4 %reduce-scatter.15.cloned.1.call-start = ((), (), s32[]{:S(2)}) async-start(), calls=%async_computation.19 | async-start | bytes 1310720 | tf_op jit(solution)/shard_map/reduce_scatter | solution.py:268
  719.7 92.0 %reduce-scatter.23.cloned.1.call-start = ((), (), s32[]{:S(2)}) async-start(), calls=%async_computation.23 | async-start | bytes 2621440 | tf_op jit(solution)/shard_map/reduce_scatter | solution.py:289
  726.6 124.0 %reduce-scatter.17.cloned.1.call-start = ((), (), s32[]{:S(2)}) async-start(), calls=%async_computation.20 | async-start | bytes 2621440 | tf_op jit(solution)/shard_map/reduce_scatter | solution.py:271
  734.4 154.4 %reduce-scatter.19.cloned.1.call-start = ((), (), s32[]{:S(2)}) async-start(), calls=%async_computation.21 | async-start | bytes 2621440 | tf_op jit(solution)/shard_map/reduce_scatter | solution.py:274
  739.8 217.9 %reduce-scatter.25.cloned.1.call-start = ((), (), s32[]{:S(2)}) async-start(), calls=%async_computation.24 | async-start | bytes 7208960 | tf_op jit(solution)/shard_map/reduce_scatter | solution.py:245
  750.8 275.8 %reduce-scatter.27.cloned.1.call-start = ((), (), s32[]{:S(2)}) async-start(), calls=%async_computation.25 | async-start | bytes 7208960 | tf_op jit(solution)/shard_map/reduce_scatter | solution.py:248
  762.0 333.6 %reduce-scatter.29.cloned.1.call-start = ((), (), s32[]{:S(2)}) async-start(), calls=%async_computation.26 | async-start | bytes 7208960 | tf_op jit(solution)/shard_map/reduce_scatter | solution.py:251
  773.4 365.9 %reduce-scatter.31.cloned.1.call-start = ((), (), s32[]{:S(2)}) async-start(), calls=%async_computation.27 | async-start | bytes 163840
  784.2 364.3 %reduce-scatter.21.cloned.1.call-start = ((), (), s32[]{:S(2)}) async-start(), calls=%async_computation.22 | async-start | bytes 40960 | tf_op jit(solution)/shard_map/reduce_scatter | solution.py:277
  785.6 507.3 %all-reduce.11.cloned.1.call-start = ((), (), s32[]{:S(2)}) async-start(), calls=%async_computation.28 | async-start | bytes 12845056 | tf_op jit(solution)/shard_map/psum | solution.py:295
  803.7 292.0 %copy-start.33 = (bf16[1024,16]{0,1:T(8,128)(2,1)S(1)}, bf16[1024,16]{0,1:T(8,128)(2,1)}, u32[]{:S(2)}) copy-start(bf16[1024,16]{0,1:T(8,128)(2,1)} %copy-done.32) | copy-start | bytes 98308
  (58 other events, 396.3 us)
Sparse Core Ops, SparseCore 0:
  9.9 29.3 all-gather.11
  41.1 26.8 all-gather.15
  69.9 35.3 all-gather.13
  106.9 35.2 all-gather.17
  144.0 35.2 all-gather.19
  181.0 65.7 all-gather.21
  248.7 65.7 all-gather.23
  316.4 65.7 all-gather.25
  714.4 27.7 reduce-scatter.12
  745.7 27.7 reduce-scatter.14
  776.5 35.1 reduce-scatter.22
  815.4 35.1 reduce-scatter.16
  853.5 35.1 reduce-scatter.18
  891.9 65.8 reduce-scatter.24
  960.9 65.7 reduce-scatter.26
  1029.8 65.7 reduce-scatter.28
  1099.0 23.8 reduce-scatter.30
  1126.0 22.4 reduce-scatter.20
  1151.5 141.4 all-reduce.10
where the time goes:
time: 1320 us; the launch traced here: 1310 us
  waiting for transfers between devices  454 us (34%)
  matrix products  359 us (27%)
  local copies, waits for them, and re-layouts  218 us (17%)
  other arithmetic  130 us (10%)
  blocking collectives  87.2 us (7%)
  loops' own time  44.2 us (3%)
  between operations  17.6 us (1%)
    psum x1, waiting for transfers between devices, local(): lax.psum(mixer_rows[1].astype(jnp.bfloat16), 'rep').astype(jnp.float32)  112 us
    dot_general x10, matrix products, right_trans(): lax.dot_general(left, right, (((1,), (1,)), ((), ())), preferred_element_...  73.3 us
    reduce_scatter x1, waiting for transfers between devices, local(): lax.psum_scatter(part_gate.astype(jnp.bfloat16), 'shard', scatter_dimensi...  69 us
    reduce_scatter x1, waiting for transfers between devices, local(): lax.psum_scatter(part_down.astype(jnp.bfloat16), 'shard', scatter_dimensi...  68.9 us
    reduce_scatter x1, waiting for transfers between devices, local(): lax.psum_scatter(part_up.astype(jnp.bfloat16), 'shard', scatter_dimension...  68.9 us
    dot_general x10, matrix products, matmul(): return jnp.dot(left, right, preferred_element_type=jnp.float32)  66.2 us
    squeeze x96, local copies, waits for them, and re-layouts, block_pass(): lax.scan(jax.checkpoint(advance), start, (shaped(query), shaped(keys), sh...  61.5 us
    dynamic_slice x80, local copies, waits for them, and re-layouts, block_pass(): lax.scan(jax.checkpoint(advance), start, (shaped(query), shaped(keys), sh...  59.3 us
  transfers between devices with their start and end apart: 19, of which 10 were waited for; matrix products, arithmetic and copies ran while one was open for 29% of the time, Pallas kernels for 0%

commit v1 on v0

--- a/solution.py
+++ b/solution.py
@@ -1,3 +1,4 @@
+import functools
 from functools import partial
 import jax
 import jax.numpy as jnp
@@ -10,6 +11,34 @@
 BLOCK = 64
 VD = 1024
 HEAD_EPS = 1.0
+
+
+def attach_array(packet, dim_k):
+    piece_out = lax.axis_index("shard")
+    mid_arr = lax.axis_size("shard")
+    piece_now, val2, then = (mid_arr, piece_out, packet.shape[dim_k])
+    line_up = [(j0, (j0 + 1) % piece_now) for j0 in range(piece_now)]
+    low = jnp.zeros(
+        (*packet.shape[:dim_k], piece_now * then, *packet.shape[dim_k + 1 :]), packet.dtype
+    )
+    low = lax.dynamic_update_slice_in_dim(low, packet, val2 * then, axis=dim_k)
+    grid = [(j0, (j0 - 1) % piece_now) for j0 in range(piece_now)]
+    mixed_arr = piece_now // 2
+    current_block = after = packet
+    for s in range(1, mixed_arr + 1):
+        current_block = lax.ppermute(current_block, "shard", line_up)
+        low = lax.dynamic_update_slice_in_dim(
+            low, current_block, (val2 - s) % piece_now * then, axis=dim_k
+        )
+        if s < piece_now - mixed_arr:
+            after = lax.ppermute(after, "shard", grid)
+            low = lax.dynamic_update_slice_in_dim(
+                low, after, (val2 + s) % piece_now * then, axis=dim_k
+            )
+    return low
+
+
+patches_manage = functools.partial(attach_array, dim_k=0)
 
 
 def matmul(left, right):
@@ -130,7 +159,7 @@
         lax.all_gather(norm_mlp, "shard", axis=0, tiled=True),
         lax.all_gather(w_gate, "shard", axis=0, tiled=True),
         lax.all_gather(w_up, "shard", axis=0, tiled=True),
-        lax.all_gather(w_down, "shard", axis=0, tiled=True),
+        patches_manage(w_down),
     )
     gain_mix, query_w, key_w, value_w, outgate_w, low_w, high_w, bias_w, headgain_w, out_w = (
         mixer_full

time: 1320 us -> 1360 us (1.030)
  waiting for transfers between devices: 454 us -> 487 us
    ppermute x0 -> x3, waiting for transfers between devices: none -> 127 us  [the longest x2 88.6 us: attach_array(): current_block = lax.ppermute(current_block, 'shard', line_up)]
    reduce_scatter x1, waiting for transfers between devices: 38.9 us -> 0.02 us  [local(): lax.psum_scatter(part_value.astype(jnp.bfloat16), 'shard', scatter_dimens...]
    reduce_scatter x1, waiting for transfers between devices: 38.2 us -> 0.02 us  [local(): lax.psum_scatter(part_outgate.astype(jnp.bfloat16), 'shard', scatter_dime...]
    unnamed x147 -> x159, local copies, waits for them, and re-layouts: 38.4 us -> 40.6 us
  transfers between devices with their start and end apart: 19 -> 22, of which waited for: 10 -> 10; matrix products, arithmetic and copies ran while one was open for 29% -> 28% of each run, Pallas kernels for 0% -> 0%
where the time goes in v1:
time: 1360 us; the launch traced here: 1350 us
  waiting for transfers between devices  487 us (36%)
  matrix products  358 us (26%)
  local copies, waits for them, and re-layouts  225 us (17%)
  other arithmetic  128 us (9%)
  blocking collectives  87.2 us (6%)
  loops' own time  44.2 us (3%)
  between operations  17.7 us (1%)
    psum x1, waiting for transfers between devices, local(): lax.psum(mixer_rows[1].astype(jnp.bfloat16), 'rep').astype(jnp.float32)  112 us
    ppermute x2, waiting for transfers between devices, attach_array(): current_block = lax.ppermute(current_block, 'shard', line_up)  88.6 us
    dot_general x10, matrix products, right_trans(): lax.dot_general(left, right, (((1,), (1,)), ((), ())), preferred_element_...  72.8 us
    reduce_scatter x1, waiting for transfers between devices, local(): lax.psum_scatter(part_down.astype(jnp.bfloat16), 'shard', scatter_dimensi...  68.9 us
    reduce_scatter x1, waiting for transfers between devices, local(): lax.psum_scatter(part_up.astype(jnp.bfloat16), 'shard', scatter_dimension...  68.9 us
    dot_general x10, matrix products, matmul(): return jnp.dot(left, right, preferred_element_type=jnp.float32)  66.5 us
    squeeze x96, local copies, waits for them, and re-layouts, block_pass(): lax.scan(jax.checkpoint(advance), start, (shaped(query), shaped(keys), sh...  61.6 us
    reduce_scatter x1, waiting for transfers between devices, local(): lax.psum_scatter(part_gate.astype(jnp.bfloat16), 'shard', scatter_dimensi...  59.7 us
  transfers between devices with their start and end apart: 22, of which 10 were waited for; matrix products, arithmetic and copies ran while one was open for 28% of the time, Pallas kernels for 0%

profile of v1, /device:TPU:0, one launch (start us, length us, event | category | flops | bytes accessed | tf_op | source)
XLA Modules:
  0.0 1352.5 jit_solution(10711363654295205862)
XLA Ops:
  18.9 9.5 all-gather
  67.2 8.9 all-reduce.1
  115.8 177.9 %while.44 = (s32[]{:T(128)}, f32[1,4,128,256]{3,2,1,0:T(8,128)S(1)}, s32[1]{0:T(128)}, f32[16,1,64,4,256]{4,2,3,1,0:T(8,128)}, f32[16,1,4,128,256]{4,3,2,1,0:T(8...) while((s32[]{:T(128)}, ...), condition=%wide.region_3.4_spmd.clone.clone, body=%wide.region_1.3_spmd.clone.sunk.clone | while | flops 280002816 | bytes 6207163 | solution.py:103
  309.2 8.6 multiply_convert_fusion.4
  326.5 11.6 fusion.159
  338.1 12.9 fusion.160
  351.0 31.3 %all-gather.26.cloned.1.call-done = bf16[2816,1024]{1,0:T(8,128)(2,1)} async-done(((bf16[704,1024]{1,0:T(8,128)(2,1)}), bf16[2816,1024]{1,0:T(8,128)(2,1)}) %all-gather.26.cloned.1.call-update) | async-done | bytes 5767184 | tf_op jit(solution)/shard_map/all_gather | solution.py:204
  382.3 21.4 %multiply_convert_fusion = (bf16[1024,2816]{1,0:T(8,128)(2,1)}, bf16[1024,2816]{1,0:T(8,128)(2,1)}, bf16[1024,2816]{1,0:T(8,128)(2,1)}) fusion(f32[1024,2816]{1,0:T(8,128)} %fusion.159, f32[1024,2816]{1,0:T(8,128)} %fusion.160, bf16[2816,1024]{1,0:T(8,128)(2,1)} %all-gather.26.cloned.1.call-done, bf16[1,1024,1024]{2,1,0:T(8,128)(2,1)S(1)} %copy-done.25), kind=kOutput, calls=%fused_computation.120 | convolution fusion | flops 5948833792 | bytes 48234496 | tf_op jit(solution)/shard_map/dot_general | solution.py:55
  403.8 10.2 fusion.161
  449.7 258.5 %while.45 = (s32[]{:T(128)}, f32[1,4,128,256]{2,3,1,0:T(8,128)S(1)}, f32[16,1,64,4,128]{4,2,3,1,0:T(8,128)}, bf16[16,1,64,4,128]{4,2,3,1,0:T(8,128)(2,1)S(1)}, b...) while((s32[]{:T(128)}, ...), condition=%wide.region_13.14_spmd.clone.clone, body=%wide.region_8.13_spmd.clone.sunk.clone | while | flops 585089280 | bytes 16077553 | solution.py:103
  738.8 10.9 convolution_convert_fusion.2
  749.7 11.1 convolution_convert_fusion.1
  761.0 11.2 convolution_convert_fusion
  776.5 47.3 %collective-permute-done = bf16[704,1024]{1,0:T(8,128)(2,1)} collective-permute-done((bf16[704,1024]{1,0:T(8,128)(2,1)S(1)}, bf16[704,1024]{1,0:T(8,128)(2,1)}, u32[]{:S(2)}, u32[]{:S(2)}) %collective-permute-start) | collective-permute-done | bytes 1441824 | tf_op jit(solution)/shard_map/ppermute | solution.py:29
  829.7 38.2 %collective-permute-done.1 = bf16[704,1024]{1,0:T(8,128)(2,1)} collective-permute-done((bf16[704,1024]{1,0:T(8,128)(2,1)S(1)}, bf16[704,1024]{1,0:T(8,128)(2,1)}, u32[]{:S(2)}, u32[]{:S(2)}) %collective-permute-start.1) | collective-permute-done | bytes 1441824 | tf_op jit(solution)/shard_map/ppermute | solution.py:34
  869.5 41.4 %collective-permute-done.2 = bf16[704,1024]{1,0:T(8,128)(2,1)} collective-permute-done((bf16[704,1024]{1,0:T(8,128)(2,1)}, bf16[704,1024]{1,0:T(8,128)(2,1)}, u32[]{:S(2)}, u32[]{:S(2)}) %collective-permute-start.2) | collective-permute-done | bytes 1441824 | tf_op jit(solution)/shard_map/ppermute | solution.py:29
  938.8 59.7 %reduce-scatter.25.cloned.1.call-done = bf16[256,2816]{1,0:T(8,128)(2,1)} async-done(((bf16[1024,2816]{1,0:T(8,128)(2,1)}), bf16[256,2816]{1,0:T(8,128)(2,1)}) %reduce-scatter.25.cloned.1.call-update) | async-done | bytes 1441808 | tf_op jit(solution)/shard_map/reduce_scatter | solution.py:274
  998.5 68.9 %reduce-scatter.27.cloned.1.call-done = bf16[256,2816]{1,0:T(8,128)(2,1)} async-done(((bf16[1024,2816]{1,0:T(8,128)(2,1)}), bf16[256,2816]{1,0:T(8,128)(2,1)}) %reduce-scatter.27.cloned.1.call-update) | async-done | bytes 1441808 | tf_op jit(solution)/shard_map/reduce_scatter | solution.py:277
  1067.4 68.9 %reduce-scatter.29.cloned.1.call-done = bf16[704,1024]{1,0:T(8,128)(2,1)} async-done(((bf16[2816,1024]{1,0:T(8,128)(2,1)}), bf16[704,1024]{1,0:T(8,128)(2,1)}) %reduce-scatter.29.cloned.1.call-update) | async-done | bytes 1441808 | tf_op jit(solution)/shard_map/reduce_scatter | solution.py:280
  1136.4 8.9 fusion.90
  1145.4 9.4 all-reduce.8
  1166.7 10.8 fusion.102
  1189.2 29.1 %all-reduce.6 = (bf16[256]{0:T(256)(128)(2,1)S(1)}, bf16[256,16]{0,1:T(8,128)(2,1)S(1)}, bf16[16,128]{1,0:T(8,128)(2,1)S(1)}, bf16[128]{0:T(256)(128)(2,1)S(1)},...) all-reduce(bf16[256]{0:T(256)(128)(2,1)S(1)} %dynamic-slice.2, ...), channel_id=1, replica_groups=mesh['rep'=8,'shard'=4] {'rep'}, use_global_device_ids=true, to_apply=%region_17.18 | all-reduce | flops 6848 | bytes 27392 | tf_op jit(solution)/shard_map/psum | solution.py:323
  1221.7 112.0 %all-reduce.11.cloned.1.call-done = (bf16[256,512]{1,0:T(8,128)(2,1)}, bf16[256,512]{1,0:T(8,128)(2,1)}, bf16[256,1024]{1,0:T(8,128)(2,1)}, bf16[256,1024]{1,0:T...) async-done(((bf16[256,512]{1,0:T(8,128)(2,1)}, bf16[256,512]{1,0:T(8,128)(2,1)}, ...) | async-done | bytes 6422544 | tf_op jit(solution)/shard_map/psum | solution.py:324
  (1024 shorter events, 648.4 us)
Async XLA Ops:
  7.2 80.9 %all-gather.12.cloned.1.call-start = ((), (), s32[]{:S(2)}) async-start(), calls=%async_computation.10 | async-start | bytes 1310720 | tf_op jit(solution)/shard_map/all_gather | solution.py:149
  7.9 82.4 %all-gather.16.cloned.1.call-start = ((), (), s32[]{:S(2)}) async-start(), calls=%async_computation.12 | async-start | bytes 1310720 | tf_op jit(solution)/shard_map/all_gather | solution.py:148
  8.7 96.6 %all-gather.14.cloned.1.call-start = ((), (), s32[]{:S(2)}) async-start(), calls=%async_computation.11 | async-start | bytes 2621440 | tf_op jit(solution)/shard_map/all_gather | solution.py:150
  9.4 299.8 %all-gather.18.cloned.1.call-start = ((), (), s32[]{:S(2)}) async-start(), calls=%async_computation.13 | async-start | bytes 2621440 | tf_op jit(solution)/shard_map/all_gather | solution.py:151
  10.0 307.9 %all-gather.20.cloned.1.call-start = ((), (), s32[]{:S(2)}) async-start(), calls=%async_computation.14 | async-start | bytes 2621440 | tf_op jit(solution)/shard_map/all_gather | solution.py:156
  10.6 314.6 %all-gather.22.cloned.1.call-start = ((), (), s32[]{:S(2)}) async-start(), calls=%async_computation.15 | async-start | bytes 7208960 | tf_op jit(solution)/shard_map/all_gather | solution.py:160
  11.1 327.0 %all-gather.24.cloned.1.call-start = ((), (), s32[]{:S(2)}) async-start(), calls=%async_computation.16 | async-start | bytes 7208960 | tf_op jit(solution)/shard_map/all_gather | solution.py:161
  11.9 370.4 %all-gather.26.cloned.1.call-start = ((), (), s32[]{:S(2)}) async-start(), calls=%async_computation.17 | async-start | bytes 7208960 | tf_op jit(solution)/shard_map/all_gather | solution.py:204
  12.6 926.1 %reduce-scatter.13.cloned.1.call-start = ((), (), s32[]{:S(2)}) async-start(), calls=%async_computation.18 | async-start | bytes 1310720 | tf_op jit(solution)/shard_map/reduce_scatter | solution.py:294
  18.4 299.4 %copy-start.2 = (bf16[1,1024,1024]{1,2,0:T(8,128)(2,1)}, bf16[1,1024,1024]{1,2,0:T(8,128)(2,1)S(1)}, u32[]{:S(2)}) copy-start(bf16[1,1024,1024]{1,2,0:T(8,128)(2,1)S(1)} %copy.180) | copy-start | bytes 6291460
  18.9 290.3 %copy-start.42 = (f32[1024]{0:T(1024)}, f32[1024]{0:T(1024)S(1)}, u32[]{:S(2)}) copy-start(f32[1024]{0:T(1024)S(1)} %fusion.144) | copy-start | bytes 12292
  714.4 224.4 %reduce-scatter.15.cloned.1.call-start = ((), (), s32[]{:S(2)}) async-start(), calls=%async_computation.19 | async-start | bytes 1310720 | tf_op jit(solution)/shard_map/reduce_scatter | solution.py:297
  718.6 220.1 %reduce-scatter.23.cloned.1.call-start = ((), (), s32[]{:S(2)}) async-start(), calls=%async_computation.23 | async-start | bytes 2621440 | tf_op jit(solution)/shard_map/reduce_scatter | solution.py:318
  725.5 213.3 %reduce-scatter.17.cloned.1.call-start = ((), (), s32[]{:S(2)}) async-start(), calls=%async_computation.20 | async-start | bytes 2621440 | tf_op jit(solution)/shard_map/reduce_scatter | solution.py:300
  733.3 205.5 %reduce-scatter.19.cloned.1.call-start = ((), (), s32[]{:S(2)}) async-start(), calls=%async_computation.21 | async-start | bytes 2621440 | tf_op jit(solution)/shard_map/reduce_scatter | solution.py:303
  738.7 259.8 %reduce-scatter.25.cloned.1.call-start = ((), (), s32[]{:S(2)}) async-start(), calls=%async_computation.24 | async-start | bytes 7208960 | tf_op jit(solution)/shard_map/reduce_scatter | solution.py:274
  749.7 317.7 %reduce-scatter.27.cloned.1.call-start = ((), (), s32[]{:S(2)}) async-start(), calls=%async_computation.25 | async-start | bytes 7208960 | tf_op jit(solution)/shard_map/reduce_scatter | solution.py:277
  760.8 375.5 %reduce-scatter.29.cloned.1.call-start = ((), (), s32[]{:S(2)}) async-start(), calls=%async_computation.26 | async-start | bytes 7208960 | tf_op jit(solution)/shard_map/reduce_scatter | solution.py:280
  772.2 408.0 %reduce-scatter.31.cloned.1.call-start = ((), (), s32[]{:S(2)}) async-start(), calls=%async_computation.27 | async-start | bytes 163840
  773.6 50.2 %collective-permute-start = (bf16[704,1024]{1,0:T(8,128)(2,1)S(1)}, bf16[704,1024]{1,0:T(8,128)(2,1)}, u32[]{:S(2)}, u32[]{:S(2)}) collective-permute-start(bf16[704,1024]{1,0:T(8,128)(2,1)S(1)} %copy-done.17), channel_id=1, source_target_pairs={{0,1},{1,2},{2,3},{3,0},{4,5},{5,6},{6,7},{7,4},{8,9},{9,10},{10,1... | collective-permute-start | bytes 4325384 | tf_op jit(solution)/shard_map/ppermute | solution.py:29
  774.9 93.0 %collective-permute-start.1 = (bf16[704,1024]{1,0:T(8,128)(2,1)S(1)}, bf16[704,1024]{1,0:T(8,128)(2,1)}, u32[]{:S(2)}, u32[]{:S(2)}) collective-permute-start(bf16[704,1024]{1,0:T(8,128)(2,1)S(1)} %copy-done.17), channel_id=1, source_target_pairs={{0,3},{1,0},{2,1},{3,2},{4,7},{5,4},{6,5},{7,6},{8,11},{9,8},{10,9... | collective-permute-start | bytes 4325384 | tf_op jit(solution)/shard_map/ppermute | solution.py:34
  823.8 87.0 %collective-permute-start.2 = (bf16[704,1024]{1,0:T(8,128)(2,1)}, bf16[704,1024]{1,0:T(8,128)(2,1)}, u32[]{:S(2)}, u32[]{:S(2)}) collective-permute-start(bf16[704,1024]{1,0:T(8,128)(2,1)} %collective-permute-done), channel_id=1, source_target_pairs={{0,1},{1,2},{2,3},{3,0},{4,5},{5,6},{6,7},{7,4},{8,9},{9,10},{10,1... | collective-permute-start | bytes 4325384 | tf_op jit(solution)/shard_map/ppermute | solution.py:29
  919.2 270.0 %reduce-scatter.21.cloned.1.call-start = ((), (), s32[]{:S(2)}) async-start(), calls=%async_computation.22 | async-start | bytes 40960 | tf_op jit(solution)/shard_map/reduce_scatter | solution.py:306
  920.7 413.1 %all-reduce.11.cloned.1.call-start = ((), (), s32[]{:S(2)}) async-start(), calls=%async_computation.28 | async-start | bytes 12845056 | tf_op jit(solution)/shard_map/psum | solution.py:324
  (67 other events, 1109.6 us)
Sparse Core Ops, SparseCore 0:
  9.9 29.4 all-gather.11
  41.2 26.8 all-gather.15
  69.9 35.3 all-gather.13
  107.0 35.2 all-gather.17
  144.0 35.2 all-gather.19
  181.1 65.8 all-gather.21
  248.8 65.7 all-gather.23
  316.5 65.7 all-gather.25
  714.5 27.6 reduce-scatter.12
  745.2 27.7 reduce-scatter.14
  776.0 52.1 reduce-scatter.22
  831.9 53.1 reduce-scatter.16
  888.1 41.3 reduce-scatter.18
  932.6 65.8 reduce-scatter.24
  1001.6 65.7 reduce-scatter.26
  1070.5 65.7 reduce-scatter.28
  1139.7 23.8 reduce-scatter.30
  1166.8 22.4 reduce-scatter.20
  1192.2 141.4 all-reduce.10
